TPU v7x, 256 devices: a whole 4x4x8 slice. The times are simulated.
256 devices in a mesh: blk: 128 (over y, z, x), rep: 2 (over core).
Axes of the slice: x: 4, y: 4, z: 8, core: 2. Of those that a mesh axis runs over, the one named last changes fastest.
Arguments:
- features: bfloat16 [32768, 256], P('blk', 'rep'), may hold values from -6 to 6
- observations: bfloat16 [256, 128], P('blk'), may hold values from -6 to 6
- cond_ids: int32 [256, 4], P('blk'), may hold values from 0 to 255, as said below
Outputs:
- block_loglik: float32 [256], P(('blk', 'rep'))
- feature_grad: float32 [32768, 256], P('blk', 'rep')
Inputs may be any that keep to these rules, and one draw needn't show every extreme that they name: `cond_ids`: row b names 4 different blocks, none of them b. Entry 0 is block (b - 1) mod 256; entry 1 is block (b - a) mod 256 for some a from 2 to 4; the remaining entries of all rows together name exactly 8 distinct blocks.
All inputs are finite; a program needn't handle non-finite values.
Results may differ from a plain program's by a relative error of at most 0.017.
Values may be sent and summed in bfloat16 or wider, within the bound.
A program may use at most 64 MiB of HBM per device.

v0:
```python
import math
import jax
import jax.numpy as jnp
from jax import lax
from jax.sharding import PartitionSpec as P

HOT = 8


def from_root(value, axis, source):
    kept = jnp.where(lax.axis_index(axis) == source, value, 0).astype(value.dtype)
    return lax.psum(kept, axis)


def from_behind(array, axis, by):
    length = lax.axis_size(axis)
    return lax.ppermute(array, axis, [(i, (i + by) % length) for i in range(length)])


def block_terms(joint_x, joint_y, own):
    joint = joint_x.shape[0]
    width = joint_x.shape[1]
    wide_x = joint_x.astype(jnp.float32)
    squares = jnp.sum(wide_x * wide_x, axis=1)
    gram = jnp.dot(joint_x, joint_x.T, preferred_element_type=jnp.float32)
    dist = squares[:, None] + squares[None, :] - 2.0 * gram
    diag_mask = jnp.eye(joint, dtype=bool)
    ident = jnp.eye(joint, dtype=jnp.float32)

    def loglik_of(dist_in):
        kern = jnp.where(diag_mask, 1.0, jnp.exp(-dist_in * (0.5 / width)))
        sigma = kern + 0.1 * ident
        chol = jnp.linalg.cholesky(sigma)
        solved = jax.scipy.linalg.solve_triangular(chol, joint_y, lower=True)
        tail = solved[joint - own :]
        logs = jnp.log(jnp.diagonal(chol)[joint - own :])
        return -0.5 * jnp.sum(tail * tail) - jnp.sum(logs) - 0.5 * own * math.log(2.0 * math.pi)

    value, pull = jax.vjp(loglik_of, dist)
    weight = pull(jnp.ones((), dist.dtype))[0]
    sym = (weight + weight.T).astype(jnp.bfloat16)
    rowsum = jnp.sum(sym.astype(jnp.float32), axis=1)
    grad = 2.0 * (
        rowsum[:, None] * wide_x - jnp.dot(sym, joint_x, preferred_element_type=jnp.float32)
    )
    return (value, grad)


def body(features, observations, cond_ids):
    per_dev = cond_ids.shape[0]
    ncond = cond_ids.shape[1]
    points = observations.shape[1]
    half = features.shape[1]
    nblocks = lax.axis_size("blk")
    device = lax.axis_index("blk")
    core = lax.axis_index("rep")
    total_blocks = per_dev * nblocks
    feat_blocks = features.reshape(per_dev, points, half)
    all_ids = jnp.arange(total_blocks, dtype=jnp.int32)
    far_ids = cond_ids[:, 2:].reshape(-1)
    marks = jnp.any(far_ids[:, None] == all_ids[None, :], axis=0).astype(jnp.int32)
    marks = lax.pmax(marks, "blk")
    order_score = marks * (2 * total_blocks) - all_ids
    unused, hot_list = lax.top_k(order_score, HOT)
    hot_owner = hot_list // per_dev
    hot_local = hot_list % per_dev
    local_ids = jnp.arange(per_dev, dtype=jnp.int32)
    owned_mask = (hot_owner == device)[:, None] & (hot_local[:, None] == local_ids[None, :])
    owned = owned_mask.astype(jnp.float32)
    feat_list = []
    obs_list = []
    for slot in range(HOT):
        piece = (feat_blocks[hot_local[slot]], observations[hot_local[slot]])
        got_feat, got_obs = (
            from_root(piece[0], "blk", hot_owner[slot]),
            from_root(piece[1], "blk", hot_owner[slot]),
        )
        feat_list.append(got_feat)
        obs_list.append(got_obs)
    hot_feat = jnp.stack(feat_list)
    hot_obs = jnp.stack(obs_list)
    near_feat = [feat_blocks]
    near_obs = [observations]
    for step_by in (1, 2):
        moved_feat, moved_obs = from_behind((feat_blocks, observations), "blk", step_by)
        near_feat.append(moved_feat)
        near_obs.append(moved_obs)
    pool_half = jnp.concatenate(near_feat + [hot_feat], axis=0)
    pool_obs = jnp.concatenate(near_obs + [hot_obs], axis=0)
    pool_full = lax.all_gather(pool_half, "rep", axis=2, tiled=True)
    width = pool_full.shape[2]
    npool = pool_full.shape[0]
    joint = (ncond + 1) * points
    near_ids = cond_ids[:, :2]
    near_slots = (device - near_ids // per_dev) % nblocks * per_dev + near_ids % per_dev
    hot_match = (cond_ids[:, 2:, None] == hot_list[None, None, :]).astype(jnp.int32)
    hot_slots = 3 * per_dev + jnp.sum(
        hot_match * jnp.arange(HOT, dtype=jnp.int32)[None, None, :], axis=2
    )
    slots = jnp.concatenate([near_slots, hot_slots, local_ids[:, None]], axis=1)
    half_count = per_dev // 2
    first_block = core * half_count
    pool_index = jnp.arange(npool, dtype=jnp.int32)

    def one_block(step, carry):
        grads, values = carry
        chosen = lax.dynamic_index_in_dim(slots, first_block + step, 0, keepdims=False)
        joint_x = pool_full[chosen].reshape(joint, width)
        joint_y = pool_obs[chosen].reshape(joint).astype(jnp.float32)
        value, grad = block_terms(joint_x, joint_y, points)
        select = (chosen[:, None] == pool_index[None, :]).astype(jnp.float32)
        grads = grads + jnp.einsum(
            "sn,spf->npf",
            select,
            grad.reshape(ncond + 1, points, width),
            precision=lax.Precision.HIGHEST,
        )
        values = values.at[step].set(value)
        return (grads, values)

    start = (jnp.zeros((npool, points, width), jnp.float32), jnp.zeros((half_count,), jnp.float32))
    pool_grad, values = lax.fori_loop(0, half_count, one_block, start)
    grad_half = lax.psum_scatter(pool_grad, "rep", scatter_dimension=2, tiled=True)
    own_grad = grad_half[:per_dev]
    for step_by in (1, 2):
        part = grad_half[step_by * per_dev : (step_by + 1) * per_dev]
        own_grad = own_grad + from_behind(part.astype(jnp.bfloat16), "blk", -step_by).astype(
            part.dtype
        )
    hot_back = lax.psum(grad_half[3 * per_dev :], "blk")
    own_grad = own_grad + jnp.einsum(
        "hb,hpf->bpf", owned, hot_back, precision=lax.Precision.HIGHEST
    )
    return (values, own_grad.reshape(per_dev * points, half))


def solution(mesh):
    placed = (P("blk", "rep"), P("blk", None), P("blk", None))
    return jax.shard_map(
        body,
        mesh=mesh,
        in_specs=placed,
        out_specs=(P(("blk", "rep")), P("blk", "rep")),
        check_vma=False,
    )
```

profile of v0, /device:TPU:2, one launch (start us, length us, event | category | flops | bytes accessed | tf_op | source)
XLA Modules:
  0.0 896.8 jit_solution(1620216628874519492)
XLA Ops:
  7.2 1.6 collective-permute-start
  8.8 2.5 collective-permute-start.1
  12.1 3.3 collective-permute-start.3
  16.5 24.8 %pmax.7 = s32[256]{0:T(256)S(1)} all-reduce(s32[256]{0:T(256)S(1)} %convert_element_type.59), channel_id=1, replica_groups=mesh['blk'=128,'rep'=2] {'blk'}, use_global_device_ids=true, to_apply=%region_1.0 | all-reduce | flops 256 | bytes 2048 | tf_op jit(solution)/shard_map/pmax | solution.py:62
  41.3 3.2 top_k.11
  66.1 1.7 dynamic-slice_select_fusion
  67.8 1.6 broadcast_select_fusion
  72.4 217.7 %all-reduce.8.cloned.1.call-done = (bf16[1,128,128]{2,1,0:T(8,128)(2,1)}, bf16[1,128,128]{2,1,0:T(8,128)(2,1)}, bf16[1,128,128]{2,1,0:T(8,128)(2,1)}, bf16[1,128...) async-done(((bf16[1,128,128]{2,1,0:T(8,128)(2,1)}, ...) | async-done | bytes 264208 | tf_op jit(solution)/shard_map/psum | solution.py:12
  296.2 2.5 all_gather.3
  299.9 2.7 broadcast_add_fusion
  302.7 1.7 copy.19
  304.4 2.6 copy.18
  307.0 2.7 add_multiply_fusion
  310.8 11.7 %cholesky.132 = f32[128,128]{1,0:T(8,128)S(1)} custom-call(f32[128,128]{1,0:T(8,128)S(1)} %cholesky.337), custom_call_target="Cholesky" | custom-call | tf_op jit(solution)/shard_map/while/body/eval_jaxpr/jvp(jit(cholesky))/cholesky | solution.py:33
  323.2 9.8 %custom-call.60 = f32[1,128,128]{1,2,0:T(8,128)S(1)} custom-call(f32[1,128,128]{2,1,0:T(8,128)S(1)} %get-tuple-element.131), custom_call_target="InvertDiagBlocksLowerTriangular" | custom-call | tf_op jit(solution)/shard_map/while/body/eval_jaxpr/jvp(jit(cholesky))/cholesky | solution.py:33
  334.4 13.2 %cholesky.270 = f32[128,128]{1,0:T(8,128)} custom-call(f32[128,128]{1,0:T(8,128)} %cholesky.341), custom_call_target="Cholesky" | custom-call | tf_op jit(solution)/shard_map/while/body/eval_jaxpr/jvp(jit(cholesky))/cholesky | solution.py:33
  347.6 2.0 select_reduce_fusion.3
  349.6 11.4 %custom-call.61 = f32[1,128,128]{1,2,0:T(8,128)} custom-call(f32[1,128,128]{2,1,0:T(8,128)} %get-tuple-element.128), custom_call_target="InvertDiagBlocksLowerTriangular" | custom-call | tf_op jit(solution)/shard_map/while/body/eval_jaxpr/jvp(jit(cholesky))/cholesky | solution.py:33
  363.3 12.5 %cholesky.291 = f32[128,128]{1,0:T(8,128)S(1)} custom-call(f32[128,128]{1,0:T(8,128)} %cholesky.346), custom_call_target="Cholesky" | custom-call | tf_op jit(solution)/shard_map/while/body/eval_jaxpr/jvp(jit(cholesky))/cholesky | solution.py:33
  375.9 1.2 select_reduce_fusion.2
  377.1 10.6 %custom-call.62 = f32[1,128,128]{1,2,0:T(8,128)S(1)} custom-call(f32[1,128,128]{2,1,0:T(8,128)} %get-tuple-element.125), custom_call_target="InvertDiagBlocksLowerTriangular" | custom-call | tf_op jit(solution)/shard_map/while/body/eval_jaxpr/jvp(jit(cholesky))/cholesky | solution.py:33
  388.5 11.9 %cholesky.310 = f32[128,128]{1,0:T(8,128)S(1)} custom-call(f32[128,128]{1,0:T(8,128)S(1)} %cholesky.351), custom_call_target="Cholesky" | custom-call | tf_op jit(solution)/shard_map/while/body/eval_jaxpr/jvp(jit(cholesky))/cholesky | solution.py:33
  400.9 9.8 %custom-call.63 = f32[1,128,128]{1,2,0:T(8,128)S(1)} custom-call(f32[1,128,128]{2,1,0:T(8,128)S(1)} %get-tuple-element.122), custom_call_target="InvertDiagBlocksLowerTriangular" | custom-call | tf_op jit(solution)/shard_map/while/body/eval_jaxpr/jvp(jit(cholesky))/cholesky | solution.py:33
  411.3 11.7 %cholesky.327 = f32[128,128]{1,0:T(8,128)S(1)} custom-call(f32[128,128]{1,0:T(8,128)S(1)} %convolution_subtract_fusion.10), custom_call_target="Cholesky" | custom-call | tf_op jit(solution)/shard_map/while/body/eval_jaxpr/jvp(jit(cholesky))/cholesky | solution.py:33
  423.1 1.4 compare_reduce_fusion.2
  424.5 1.4 compare_reduce_fusion.1
  426.5 1.4 concatenate.95
  428.6 1.3 compare_reduce_fusion.3
  433.0 1.4 fusion.11
  434.5 14.4 %while.3 = (s32[]{:T(128)}, f32[640,640]{1,0:T(8,128)}, s32[5,2]{0,1:T(2,128)S(1)}, f32[5,128,128]{2,1,0:T(8,128)S(1)}, s32[]{:T(128)}) while((s32[]{:T(128)}, f32[640,640]{1,0:T(8,128)}, s32[5,2]{0,1:T(2,128)S(1)}, f32[5,128,128]{2,1,0:T(8,128)S(1)}, s32[]{:T(128)}) %tuple.109), condition=%wide.while_cond.1, body=%wide.while_body.1.sunk | while | flops 2 | bytes 131189 | solution.py:34
  435.1 2.3 bitcast_dynamic-update-slice_fusion.4
  438.0 2.3 bitcast_dynamic-update-slice_fusion.4
  440.9 2.3 bitcast_dynamic-update-slice_fusion.4
  443.8 2.3 bitcast_dynamic-update-slice_fusion.4
  446.7 2.2 bitcast_dynamic-update-slice_fusion.4
  448.9 49.1 %custom-call.64 = f32[5,128,128]{1,2,0:T(8,128)S(1)} custom-call(f32[5,128,128]{2,1,0:T(8,128)S(1)} %get-tuple-element.65), custom_call_target="InvertDiagBlocksLowerTriangular" | custom-call | tf_op jit(solution)/shard_map/while/body/eval_jaxpr/jvp(jit(_solve_triangular))/triangular_solve | solution.py:34
  502.1 1.2 convolution_bitcast_fusion.1
  504.2 5.8 gather_fusion.2
  514.7 1.2 fusion.43
  516.5 34.9 %scatter_fusion = f32[640,640]{1,0:T(8,128)S(1)} fusion(f32[640,640]{1,0:T(8,128)S(1)} %negate_select_fusion, s32[640]{0:T(1024)S(1)} %get-tuple-element.183, f32[640]{0:T(1024)S(1)} %pad.10), kind=kCustom, calls=%fused_computation.3 | custom fusion | flops 640 | bytes 12800 | tf_op jit(solution)/shard_map/while/body/eval_jaxpr/transpose(jvp(jit(diagonal)))/cond/branch_0_fun/scatter-add | solution.py:36
  551.4 7.3 divide_select_fusion
  558.7 9.6 %while.4 = (s32[]{:T(128)}, f32[640,640]{1,0:T(8,128)S(1)}, s32[5,2]{0,1:T(2,128)S(1)}, f32[5,128,128]{2,1,0:T(8,128)S(1)}, s32[]{:T(128)}) while((s32[]{:T(128)}, f32[640,640]{1,0:T(8,128)S(1)}, s32[5,2]{0,1:T(2,128)S(1)}, f32[5,128,128]{2,1,0:T(8,128)S(1)}, s32[]{:T(128)}) %tuple.122), condition=%wide.while_cond.2, body=%wide.while_body.2.sunk | while | flops 2 | bytes 131189 | solution.py:33
  559.3 1.3 bitcast_dynamic-update-slice_fusion.5
  561.2 1.3 bitcast_dynamic-update-slice_fusion.5
  563.1 1.3 bitcast_dynamic-update-slice_fusion.5
  565.1 1.3 bitcast_dynamic-update-slice_fusion.5
  567.0 1.3 bitcast_dynamic-update-slice_fusion.5
  568.3 49.3 %custom-call.65 = f32[5,128,128]{1,2,0:T(8,128)S(1)} custom-call(f32[5,128,128]{2,1,0:T(8,128)S(1)} %get-tuple-element.73), custom_call_target="InvertDiagBlocksLowerTriangular" | custom-call | tf_op jit(solution)/shard_map/while/body/eval_jaxpr/transpose(jvp(jit(cholesky)))/triangular_solve | solution.py:33
  617.6 1.5 fusion.71
  619.1 1.4 convolution_subtract_fusion.4
  628.2 1.8 convolution_subtract_fusion.5
  630.5 2.4 fusion.31
  634.6 1.5 fusion.6
  636.1 2.9 copy.21
  639.0 3.6 fusion.4
  642.6 2.2 copy.22
  646.2 2.8 fusion.46
  649.1 13.7 %reduce-scatter.2.cloned.1.call-done = f32[14,128,128]{2,0,1:T(8,128)} async-done(((f32[14,128,256]{2,0,1:T(8,128)}), f32[14,128,128]{2,0,1:T(8,128)}) %reduce-scatter.2.cloned.1.call-update) | async-done | bytes 917520 | tf_op jit(solution)/shard_map/reduce_scatter | solution.py:123
  662.8 2.2 slice.521
  665.2 7.1 collective-permute-start.5
  672.3 1.5 collective-permute-start.4
  675.1 1.5 collective-permute-done.4
  676.6 210.2 %all-reduce.6.cloned.1.call-done = f32[8,128,128]{2,0,1:T(8,128)} async-done(((f32[8,128,128]{2,0,1:T(8,128)}), f32[8,128,128]{2,0,1:T(8,128)}) %all-reduce.6.cloned.1.call-update) | async-done | bytes 524304 | tf_op jit(solution)/shard_map/psum | solution.py:130
  886.8 1.4 fusion.87
  (178 shorter events, 51.2 us)
Async XLA Ops:
  7.2 282.9 %all-reduce.8.cloned.1.call-start = ((), (), s32[]{:S(2)}) async-start(), calls=%async_computation.3 | async-start | bytes 532480 | tf_op jit(solution)/shard_map/psum | solution.py:12
  7.2 65.1 %collective-permute-start = (bf16[2,128,128]{2,1,0:T(8,128)(2,1)}, bf16[2,128,128]{2,1,0:T(8,128)(2,1)S(1)}, u32[]{:S(2)}, u32[]{:S(2)}) collective-permute-start(bf16[2,128,128]{2,1,0:T(8,128)(2,1)} %bitcast.322), channel_id=1, source_target_pairs={{0,2},{2,4},{4,6},{6,8},{8,10},{10,12},{12,14},{14,16},{16,18},{18... | collective-permute-start | bytes 196616 | tf_op jit(solution)/shard_map/ppermute | solution.py:17
  8.8 63.6 %collective-permute-start.1 = (bf16[2,128,128]{2,1,0:T(8,128)(2,1)}, bf16[2,128,128]{2,1,0:T(8,128)(2,1)S(1)}, u32[]{:S(2)}, u32[]{:S(2)}) collective-permute-start(bf16[2,128,128]{2,1,0:T(8,128)(2,1)} %bitcast.323), channel_id=1, source_target_pairs={{0,4},{2,6},{4,8},{6,10},{8,12},{10,14},{12,16},{14,18},{16,20},{1... | collective-permute-start | bytes 196616 | tf_op jit(solution)/shard_map/ppermute | solution.py:17
  11.2 415.2 %collective-permute-start.2 = (bf16[2,128]{1,0:T(2,128)(2,1)}, bf16[2,128]{1,0:T(2,128)(2,1)}, u32[]{:S(2)}, u32[]{:S(2)}) collective-permute-start(bf16[2,128]{1,0:T(2,128)(2,1)} %param.6), channel_id=1, source_target_pairs={{0,2},{2,4},{4,6},{6,8},{8,10},{10,12},{12,14},{14,16},{16,18},{18... | collective-permute-start | bytes 1544 | tf_op jit(solution)/shard_map/ppermute | solution.py:17
  12.1 414.4 %collective-permute-start.3 = (bf16[2,128]{1,0:T(2,128)(2,1)}, bf16[2,128]{1,0:T(2,128)(2,1)}, u32[]{:S(2)}, u32[]{:S(2)}) collective-permute-start(bf16[2,128]{1,0:T(2,128)(2,1)} %param.6), channel_id=1, source_target_pairs={{0,4},{2,6},{4,8},{6,10},{8,12},{10,14},{12,16},{14,18},{16,20},{1... | collective-permute-start | bytes 1544 | tf_op jit(solution)/shard_map/ppermute | solution.py:17
  69.3 593.5 %reduce-scatter.2.cloned.1.call-start = ((), (), s32[]{:S(2)}) async-start(), calls=%async_computation.1 | async-start | bytes 3145728 | tf_op jit(solution)/shard_map/reduce_scatter | solution.py:123
  71.7 227.7 %copy-start.14 = (s32[1024]{0:T(1024)}, s32[1024]{0:T(1024)S(1)}, u32[]{:S(2)}) copy-start(s32[1024]{0:T(1024)S(1)} %pad_clamp_fusion) | copy-start | bytes 12292
  299.2 0.7 copy-start.6
  302.7 4.3 copy-start
  306.9 2.7 copy-start.2
  309.6 1.2 copy-start.8
  310.8 22.2 %copy-start.9 = (f32[640,640]{1,0:T(8,128)S(1)}, f32[640,640]{1,0:T(8,128)}, u32[]{:S(2)}) copy-start(f32[640,640]{1,0:T(8,128)} %copy-done.8) | copy-start | bytes 4915204
  362.2 64.3 %copy-start.12 = (bf16[2,128]{1,0:T(2,128)(2,1)S(1)}, bf16[2,128]{1,0:T(2,128)(2,1)}, u32[]{:S(2)}) copy-start(bf16[2,128]{1,0:T(2,128)(2,1)} %param.6) | copy-start | bytes 1540
  423.1 11.3 %copy-start.5 = (f32[640,640]{1,0:T(8,128)}, f32[640,640]{1,0:T(8,128)S(1)}, u32[]{:S(2)}) copy-start(f32[640,640]{1,0:T(8,128)S(1)} %get-tuple-element.120) | copy-start | bytes 4915204
  433.0 1.4 copy-start.17
  617.6 3.4 copy-start.11
  633.5 1.1 copy-start.13
  636.1 2.9 copy-start.1
  636.1 2.9 copy-start.3
  642.6 2.2 copy-start.4
  644.8 1.0 copy-start.7
  645.1 1.2 copy-start.16
  649.0 237.8 %copy-start.15 = (pred[8]{0:T(512)(128)(4,1)S(1)}, pred[8]{0:T(512)(128)(4,1)}, u32[]{:S(2)}) copy-start(pred[8]{0:T(512)(128)(4,1)} %get-tuple-element.106) | copy-start | bytes 28
  649.0 237.7 %all-reduce.6.cloned.1.call-start = ((), (), s32[]{:S(2)}) async-start(), calls=%async_computation.2 | async-start | bytes 1048576 | tf_op jit(solution)/shard_map/psum | solution.py:130
  662.8 2.2 copy-start.10
  665.2 9.9 %collective-permute-start.5 = (bf16[2,128,128]{2,0,1:T(2,128)(2,1)S(1)}, bf16[2,128,128]{2,0,1:T(2,128)(2,1)S(1)}, u32[]{:S(2)}, u32[]{:S(2)}) collective-permute-start(bf16[2,128,128]{2,0,1:T(2,128)(2,1)S(1)} %get-tuple-element.118), channel_id=1, source_target_pairs={{0,252},{2,254},{4,0},{6,2},{8,4},{10,6},{12,8},{14,10},{16,12},{1... | collective-permute-start | bytes 196616 | tf_op jit(solution)/shard_map/ppermute | solution.py:17
  672.3 4.3 collective-permute-start.4
Sparse Core Ops, SparseCore 0:
  69.5 220.5 all-reduce.7
  649.1 13.6 reduce-scatter.1
  669.1 217.6 all-reduce.5
where the time goes:
time: 904 us; the launch traced here: 897 us
  waiting for transfers between devices  443 us (49%)
  other arithmetic  265 us (29%)
  local copies, waits for them, and re-layouts  58.9 us (7%)
  matrix products  45.5 us (5%)
  between operations  40 us (4%)
  blocking collectives  27.3 us (3%)
  starting transfers between devices  16.9 us (2%)
    psum x1, waiting for transfers between devices, from_root(): return lax.psum(kept, axis)  218 us
    psum x1, waiting for transfers between devices, body(): hot_back = lax.psum(grad_half[3 * per_dev:], 'blk')  210 us
    another operation x20, other arithmetic, loglik_of(): chol = jnp.linalg.cholesky(sigma)  162 us
    another operation x4, other arithmetic, loglik_of(): solved = jax.scipy.linalg.solve_triangular(chol, joint_y, lower=True)  50.6 us
    scatter-add x1, other arithmetic, loglik_of(): logs = jnp.log(jnp.diagonal(chol)[joint - own:])  34.9 us
    pmax x1, blocking collectives, body(): marks = lax.pmax(marks, 'blk')  24.8 us
    another operation x30, local copies, waits for them, and re-layouts  23.8 us
    another operation x26, matrix products, loglik_of(): chol = jnp.linalg.cholesky(sigma)  19.2 us
  transfers between devices with their start and end apart: 9, of which 4 were waited for; matrix products, arithmetic and copies ran while one was open for 16% of the time, Pallas kernels for 0%

commit v1 on v0

--- a/solution.py
+++ b/solution.py
@@ -9,7 +9,7 @@
 
 def from_root(value, axis, source):
     kept = jnp.where(lax.axis_index(axis) == source, value, 0).astype(value.dtype)
-    return lax.psum(kept, axis)
+    return jnp.sum(lax.all_gather(kept, axis), axis=0)
 
 
 def from_behind(array, axis, by):

time: 904 us -> 3410 us (3.77)
  blocking collectives: 27.3 us -> 2740 us
  waiting for transfers between devices: 443 us -> 223 us
    all_gather x0 -> x8, blocking collectives: none -> 2700 us  [from_root(): return jnp.sum(lax.all_gather(kept, axis), axis=0)]
    psum x1 -> x0, waiting for transfers between devices: 218 us -> none  [from_root(): return lax.psum(kept, axis)]
  transfers between devices with their start and end apart: 9 -> 16, of which waited for: 4 -> 3; matrix products, arithmetic and copies ran while one was open for 16% -> 1% of each run, Pallas kernels for 0% -> 0%
where the time goes in v1:
time: 3410 us; the launch traced here: 3400 us
  blocking collectives  2740 us (80%)
  other arithmetic  289 us (8%)
  waiting for transfers between devices  223 us (7%)
  local copies, waits for them, and re-layouts  49.2 us (1%)
  matrix products  45.5 us (1%)
  between operations  40.8 us (1%)
    all_gather x8, blocking collectives, from_root(): return jnp.sum(lax.all_gather(kept, axis), axis=0)  2700 us
    psum x1, waiting for transfers between devices, body(): hot_back = lax.psum(grad_half[3 * per_dev:], 'blk')  210 us
    another operation x20, other arithmetic, loglik_of(): chol = jnp.linalg.cholesky(sigma)  162 us
  transfers between devices with their start and end apart: 16, of which 3 were waited for; matrix products, arithmetic and copies ran while one was open for 1% of the time, Pallas kernels for 0%

profile of v1, /device:TPU:2, one launch (start us, length us, event | category | flops | bytes accessed | tf_op | source)
XLA Modules:
  0.0 3398.1 jit_solution(12022784940022070048)
XLA Ops:
  8.2 30.2 pmax.7
  38.4 3.2 top_k.11
  63.4 1.7 dynamic-slice_select_fusion
  70.0 3.9 collective-permute-start.1
  73.9 2.6 collective-permute-start.3
  77.5 336.5 %all-gather = bf16[128,1,128]{2,1,0:T(2,128)(2,1)S(1)} all-gather(bf16[1,1,128]{2,1,0:T(2,128)(2,1)S(1)} %get-tuple-element.137), channel_id=1, replica_groups=mesh['blk'=128,'rep'=2] {'blk'}, dimensions={0}, use_global_device_ids=true | all-gather | bytes 33024 | tf_op jit(solution)/shard_map/all_gather | solution.py:12
  414.0 342.2 %all-gather.1 = bf16[128,1,128]{2,1,0:T(2,128)(2,1)S(1)} all-gather(bf16[1,1,128]{2,1,0:T(2,128)(2,1)S(1)} %get-tuple-element.136), channel_id=1, replica_groups=mesh['blk'=128,'rep'=2] {'blk'}, dimensions={0}, use_global_device_ids=true | all-gather | bytes 33024 | tf_op jit(solution)/shard_map/all_gather | solution.py:12
  756.3 336.2 %all-gather.2 = bf16[128,1,128]{2,1,0:T(2,128)(2,1)S(1)} all-gather(bf16[1,1,128]{2,1,0:T(2,128)(2,1)S(1)} %get-tuple-element.135), channel_id=1, replica_groups=mesh['blk'=128,'rep'=2] {'blk'}, dimensions={0}, use_global_device_ids=true | all-gather | bytes 33024 | tf_op jit(solution)/shard_map/all_gather | solution.py:12
  1092.5 338.2 %all-gather.3 = bf16[128,1,128]{2,1,0:T(2,128)(2,1)S(1)} all-gather(bf16[1,1,128]{2,1,0:T(2,128)(2,1)S(1)} %get-tuple-element.134), channel_id=1, replica_groups=mesh['blk'=128,'rep'=2] {'blk'}, dimensions={0}, use_global_device_ids=true | all-gather | bytes 33024 | tf_op jit(solution)/shard_map/all_gather | solution.py:12
  1430.7 336.2 %all-gather.4 = bf16[128,1,128]{2,1,0:T(2,128)(2,1)S(1)} all-gather(bf16[1,1,128]{2,1,0:T(2,128)(2,1)S(1)} %get-tuple-element.133), channel_id=1, replica_groups=mesh['blk'=128,'rep'=2] {'blk'}, dimensions={0}, use_global_device_ids=true | all-gather | bytes 33024 | tf_op jit(solution)/shard_map/all_gather | solution.py:12
  1766.8 338.2 %all-gather.5 = bf16[128,1,128]{2,1,0:T(2,128)(2,1)S(1)} all-gather(bf16[1,1,128]{2,1,0:T(2,128)(2,1)S(1)} %get-tuple-element.132), channel_id=1, replica_groups=mesh['blk'=128,'rep'=2] {'blk'}, dimensions={0}, use_global_device_ids=true | all-gather | bytes 33024 | tf_op jit(solution)/shard_map/all_gather | solution.py:12
  2105.0 336.2 %all-gather.6 = bf16[128,1,128]{2,1,0:T(2,128)(2,1)S(1)} all-gather(bf16[1,1,128]{2,1,0:T(2,128)(2,1)S(1)} %get-tuple-element.131), channel_id=1, replica_groups=mesh['blk'=128,'rep'=2] {'blk'}, dimensions={0}, use_global_device_ids=true | all-gather | bytes 33024 | tf_op jit(solution)/shard_map/all_gather | solution.py:12
  2441.2 338.7 %all-gather.7 = bf16[128,1,128]{2,1,0:T(2,128)(2,1)S(1)} all-gather(bf16[1,1,128]{2,1,0:T(2,128)(2,1)S(1)} %get-tuple-element.130), channel_id=1, replica_groups=mesh['blk'=128,'rep'=2] {'blk'}, dimensions={0}, use_global_device_ids=true | all-gather | bytes 33024 | tf_op jit(solution)/shard_map/all_gather | solution.py:12
  2784.0 2.8 reduce_sum.241
  2786.9 2.8 reduce_sum.242
  2789.7 2.8 reduce_sum.243
  2792.6 2.8 reduce_sum.244
  2795.4 2.8 reduce_sum.245
  2798.3 2.8 reduce_sum.246
  2801.1 2.8 reduce_sum.247
  2804.1 2.8 reduce_sum.248
  2806.9 2.5 all_gather.75
  2810.7 2.7 broadcast_add_fusion
  2813.4 1.7 copy.26
  2815.1 2.3 copy.25
  2817.4 2.7 add_multiply_fusion
  2821.3 11.7 cholesky.132
  2833.6 9.8 custom-call.60
  2844.8 13.2 cholesky.270
  2858.0 2.1 select_reduce_fusion.3
  2860.1 11.5 custom-call.61
  2873.8 12.5 cholesky.291
  2887.6 10.6 custom-call.62
  2899.0 12.1 cholesky.310
  2911.6 9.8 custom-call.63
  2922.0 11.7 cholesky.327
  2941.7 1.4 fusion.11
  2943.1 14.0 while.3
  2943.7 2.2 bitcast_dynamic-update-slice_fusion.4
  2946.6 2.2 bitcast_dynamic-update-slice_fusion.4
  2949.4 2.2 bitcast_dynamic-update-slice_fusion.4
  2952.2 2.2 bitcast_dynamic-update-slice_fusion.4
  2955.0 2.1 bitcast_dynamic-update-slice_fusion.4
  2957.2 49.1 %custom-call.64 = f32[5,128,128]{1,2,0:T(8,128)S(1)} custom-call(f32[5,128,128]{2,1,0:T(8,128)S(1)} %get-tuple-element.65), custom_call_target="InvertDiagBlocksLowerTriangular" | custom-call | tf_op jit(solution)/shard_map/while/body/eval_jaxpr/jvp(jit(_solve_triangular))/triangular_solve | solution.py:34
  3012.5 5.6 gather_fusion.2
  3024.6 34.9 %scatter_fusion = f32[640,640]{1,0:T(8,128)S(1)} fusion(f32[640,640]{1,0:T(8,128)S(1)} %negate_select_fusion, s32[640]{0:T(1024)S(1)} %get-tuple-element.167, f32[640]{0:T(1024)S(1)} %pad.10), kind=kCustom, calls=%fused_computation.3 | custom fusion | flops 640 | bytes 12800 | tf_op jit(solution)/shard_map/while/body/eval_jaxpr/transpose(jvp(jit(diagonal)))/cond/branch_0_fun/scatter-add | solution.py:36
  3059.5 7.3 divide_select_fusion
  3066.8 9.1 while.4
  3075.9 49.3 %custom-call.65 = f32[5,128,128]{1,2,0:T(8,128)S(1)} custom-call(f32[5,128,128]{2,1,0:T(8,128)S(1)} %get-tuple-element.73), custom_call_target="InvertDiagBlocksLowerTriangular" | custom-call | tf_op jit(solution)/shard_map/while/body/eval_jaxpr/transpose(jvp(jit(cholesky)))/triangular_solve | solution.py:33
  3125.2 1.5 fusion.71
  3126.8 1.4 convolution_subtract_fusion.4
  3135.8 1.8 convolution_subtract_fusion.5
  3138.1 2.5 fusion.31
  3142.2 1.5 fusion.6
  3143.8 2.9 copy.28
  3146.7 3.6 fusion.4
  3150.2 2.2 copy.29
  3153.9 2.8 fusion.46
  3156.7 7.2 reduce-scatter.2.cloned.1.call-done
  3163.9 2.2 slice.521
  3166.4 7.1 collective-permute-start.5
  3173.5 1.4 collective-permute-start.4
  3176.2 1.5 collective-permute-done.4
  3177.7 210.0 %all-reduce.4.cloned.1.call-done = f32[8,128,128]{2,0,1:T(8,128)} async-done(((f32[8,128,128]{2,0,1:T(8,128)}), f32[8,128,128]{2,0,1:T(8,128)}) %all-reduce.4.cloned.1.call-update) | async-done | bytes 524304 | tf_op jit(solution)/shard_map/psum | solution.py:130
  (227 shorter events, 65.6 us)
Async XLA Ops:
  7.2 2774.2 %copy-start.11 = (bf16[256,128]{1,0:T(8,128)(2,1)S(1)}, bf16[256,128]{1,0:T(8,128)(2,1)}, u32[]{:S(2)}) copy-start(bf16[256,128]{1,0:T(8,128)(2,1)} %param.5) | copy-start | bytes 196612
  7.2 2776.1 %copy-start.13 = (bf16[2,128]{1,0:T(2,128)(2,1)S(1)}, bf16[2,128]{1,0:T(2,128)(2,1)}, u32[]{:S(2)}) copy-start(bf16[2,128]{1,0:T(2,128)(2,1)} %param.6) | copy-start | bytes 1540
  7.2 2776.8 %all-gather.17.cloned.1.call-start = ((), (), s32[]{:S(2)}) async-start(), calls=%async_computation.1 | async-start | bytes 4227072 | tf_op jit(solution)/shard_map/all_gather | solution.py:12
  65.1 2721.7 %all-gather.19.cloned.1.call-start = ((), (), s32[]{:S(2)}) async-start(), calls=%async_computation.2 | async-start | bytes 4227072 | tf_op jit(solution)/shard_map/all_gather | solution.py:12
  65.9 2723.8 %all-gather.21.cloned.1.call-start = ((), (), s32[]{:S(2)}) async-start(), calls=%async_computation.3 | async-start | bytes 4227072 | tf_op jit(solution)/shard_map/all_gather | solution.py:12
  66.6 2726.0 %all-gather.23.cloned.1.call-start = ((), (), s32[]{:S(2)}) async-start(), calls=%async_computation.4 | async-start | bytes 4227072 | tf_op jit(solution)/shard_map/all_gather | solution.py:12
  67.2 2728.2 %all-gather.25.cloned.1.call-start = ((), (), s32[]{:S(2)}) async-start(), calls=%async_computation.5 | async-start | bytes 4227072 | tf_op jit(solution)/shard_map/all_gather | solution.py:12
  67.8 2730.5 %all-gather.27.cloned.1.call-start = ((), (), s32[]{:S(2)}) async-start(), calls=%async_computation.6 | async-start | bytes 4227072 | tf_op jit(solution)/shard_map/all_gather | solution.py:12
  68.3 2732.8 %all-gather.29.cloned.1.call-start = ((), (), s32[]{:S(2)}) async-start(), calls=%async_computation.7 | async-start | bytes 4227072 | tf_op jit(solution)/shard_map/all_gather | solution.py:12
  69.1 2735.0 %all-gather.31.cloned.1.call-start = ((), (), s32[]{:S(2)}) async-start(), calls=%async_computation.8 | async-start | bytes 4227072 | tf_op jit(solution)/shard_map/all_gather | solution.py:12
  69.8 3094.1 %reduce-scatter.2.cloned.1.call-start = ((), (), s32[]{:S(2)}) async-start(), calls=%async_computation.9 | async-start | bytes 3145728 | tf_op jit(solution)/shard_map/reduce_scatter | solution.py:123
  69.9 2714.0 %collective-permute-start = (bf16[2,128,128]{2,1,0:T(8,128)(2,1)}, bf16[2,128,128]{2,1,0:T(8,128)(2,1)S(1)}, u32[]{:S(2)}, u32[]{:S(2)}) collective-permute-start(bf16[2,128,128]{2,1,0:T(8,128)(2,1)} %bitcast.363), channel_id=1, source_target_pairs={{0,2},{2,4},{4,6},{6,8},{8,10},{10,12},{12,14},{14,16},{16,18},{18... | collective-permute-start | bytes 196616 | tf_op jit(solution)/shard_map/ppermute | solution.py:17
  70.0 2714.0 %collective-permute-start.1 = (bf16[2,128,128]{2,1,0:T(8,128)(2,1)}, bf16[2,128,128]{2,1,0:T(8,128)(2,1)S(1)}, u32[]{:S(2)}, u32[]{:S(2)}) collective-permute-start(bf16[2,128,128]{2,1,0:T(8,128)(2,1)} %bitcast.364), channel_id=1, source_target_pairs={{0,4},{2,6},{4,8},{6,10},{8,12},{10,14},{12,16},{14,18},{16,20},{1... | collective-permute-start | bytes 196616 | tf_op jit(solution)/shard_map/ppermute | solution.py:17
  73.9 2709.3 %collective-permute-start.2 = (bf16[2,128]{1,0:T(2,128)(2,1)}, bf16[2,128]{1,0:T(2,128)(2,1)S(1)}, u32[]{:S(2)}, u32[]{:S(2)}) collective-permute-start(bf16[2,128]{1,0:T(2,128)(2,1)} %param.6), channel_id=1, source_target_pairs={{0,2},{2,4},{4,6},{6,8},{8,10},{10,12},{12,14},{14,16},{16,18},{18... | collective-permute-start | bytes 1544 | tf_op jit(solution)/shard_map/ppermute | solution.py:17
  73.9 2709.3 %collective-permute-start.3 = (bf16[2,128]{1,0:T(2,128)(2,1)}, bf16[2,128]{1,0:T(2,128)(2,1)S(1)}, u32[]{:S(2)}, u32[]{:S(2)}) collective-permute-start(bf16[2,128]{1,0:T(2,128)(2,1)} %param.6), channel_id=1, source_target_pairs={{0,4},{2,6},{4,8},{6,10},{8,12},{10,14},{12,16},{14,18},{16,20},{1... | collective-permute-start | bytes 1544 | tf_op jit(solution)/shard_map/ppermute | solution.py:17
  2783.9 2.9 copy-start.14
  2809.9 0.7 copy-start.6
  2813.4 4.0 copy-start
  2817.4 2.7 copy-start.2
  2820.1 1.2 copy-start.8
  2821.3 22.2 copy-start.9
  2933.8 9.3 copy-start.5
  2941.7 1.4 copy-start.19
  2941.7 64.7 %copy-start.15 = (bf16[5,128]{1,0:T(8,128)(2,1)S(1)}, bf16[5,128]{1,0:T(8,128)(2,1)}, u32[]{:S(2)}) copy-start(bf16[5,128]{1,0:T(8,128)(2,1)} %copy-done.14) | copy-start | bytes 3844
  3125.2 3.4 copy-start.12
  3141.1 1.1 copy-start.16
  3143.8 2.9 copy-start.1
  3143.8 2.9 copy-start.3
  3150.2 2.2 copy-start.4
  3152.5 1.0 copy-start.7
  3152.7 1.2 copy-start.18
  3156.7 231.0 %copy-start.17 = (pred[8]{0:T(512)(128)(4,1)S(1)}, pred[8]{0:T(512)(128)(4,1)}, u32[]{:S(2)}) copy-start(pred[8]{0:T(512)(128)(4,1)} %get-tuple-element.90) | copy-start | bytes 28
  3156.7 231.0 %all-reduce.4.cloned.1.call-start = ((), (), s32[]{:S(2)}) async-start(), calls=%async_computation.10 | async-start | bytes 1048576 | tf_op jit(solution)/shard_map/psum | solution.py:130
  3163.9 2.2 copy-start.10
  3166.4 9.8 collective-permute-start.5
  3173.5 4.3 collective-permute-start.4
Sparse Core Ops, SparseCore 0:
  65.2 111.1 all-gather.16
  180.0 113.9 all-gather.18
  297.6 113.9 all-gather.20
  415.0 113.9 all-gather.22
  532.5 113.7 all-gather.24
  649.8 113.8 all-gather.26
  767.3 113.9 all-gather.28
  885.4 113.9 all-gather.30
  3156.8 7.0 reduce-scatter.1
  3170.1 217.5 all-reduce.3
